TPU v7x, 32 devices: a whole 2x2x4 slice. The times are simulated.
32 devices in a mesh: blk: 4 (over y, x), rep: 8 (over z, core).
Axes of the slice: x: 2, y: 2, z: 4, core: 2. Of those that a mesh axis runs over, the one named last changes fastest.
Arguments:
- image_feats: bfloat16 [8, 2048, 1024], P('rep', 'blk'), may hold values from -6 to 6
- text_feats: bfloat16 [8, 2048, 768], P('rep', 'blk'), may hold values from -6 to 6
- image_head: bfloat16 [1024, 768], replicated, may hold values from -0.1875 to 0.1875
- text_head: bfloat16 [768, 768], replicated, may hold values from -0.21875 to 0.21875
- image_lse: float32 [8, 2048], P('rep', 'blk'), as said below
- text_lse: float32 [8, 2048], P('rep', 'blk'), as said below
Outputs:
- image_feat_grad: float32 [8, 2048, 1024], P('rep', 'blk')
- text_feat_grad: float32 [8, 2048, 768], P('rep', 'blk')
- image_head_grad: float32 [1024, 768], replicated
- text_head_grad: float32 [768, 768], replicated
Inputs may be any that keep to these rules, and one draw needn't show every extreme that they name: `image_lse`: each entry lies between ln(2048) + 1 and ln(2048) + 2.5. `text_lse`: each entry lies between ln(2048) + 1 and ln(2048) + 2.5.
All inputs are finite; a program needn't handle non-finite values.
Results may differ from a plain program's by a relative error of at most 0.028.
Values may be sent and summed in bfloat16 or wider, within the bound.
A program may use at most 128 MiB of HBM per device.

v0:
```python
import jax
import jax.numpy as jnp
from jax import lax
from jax.sharding import PartitionSpec as P

logit_scale = 50.0
epsilon = 1e-06


def project_head(feats, weight):
    raw = jnp.dot(feats, weight, preferred_element_type=jnp.float32)
    factor = lax.rsqrt(jnp.sum(raw * raw, axis=1, keepdims=True) + epsilon)
    return (raw * factor, factor)


def pre_gradient(embed, factor, grad):
    inner = jnp.sum(embed * grad, axis=1, keepdims=True)
    return (factor * (grad - embed * inner)).astype(jnp.bfloat16)


def weight_tile(left, left_lse, right, right_lse):
    scores = logit_scale * lax.dot_general(
        left, right, (((1,), (1,)), ((), ())), preferred_element_type=jnp.float32
    )
    return (
        0.5 * (jnp.exp(scores - left_lse[:, None]) + jnp.exp(scores - right_lse[None, :]))
    ).astype(jnp.bfloat16)


def shards(image_feats, text_feats, image_head, text_head, image_lse, text_lse):
    image_rows = image_feats[0]
    text_rows = text_feats[0]
    lse_img = image_lse[0]
    lse_txt = text_lse[0]
    image_embed, image_scale = project_head(image_rows, image_head)
    text_embed, text_scale = project_head(text_rows, text_head)
    image_round = image_embed.astype(jnp.bfloat16)
    text_round = text_embed.astype(jnp.bfloat16)
    image_piece = lax.all_gather(image_round, "blk", axis=0, tiled=True)
    image_piece_lse = lax.all_gather(
        lse_img.astype(jnp.bfloat16), "blk", axis=0, tiled=True
    ).astype(jnp.float32)
    text_piece = lax.all_gather(text_round, "blk", axis=0, tiled=True)
    text_piece_lse = lax.all_gather(lse_txt.astype(jnp.bfloat16), "blk", axis=0, tiled=True).astype(
        jnp.float32
    )
    image_weights = weight_tile(image_round, lse_img, text_piece, text_piece_lse)
    image_total_part = jnp.dot(image_weights, text_piece, preferred_element_type=jnp.float32)
    text_weights = weight_tile(image_piece, image_piece_lse, text_round, lse_txt)
    text_total_part = lax.dot_general(
        text_weights, image_piece, (((0,), (0,)), ((), ())), preferred_element_type=jnp.float32
    )
    image_grad = logit_scale * image_total_part - logit_scale * text_round.astype(jnp.float32)
    text_grad = logit_scale * text_total_part - logit_scale * image_round.astype(jnp.float32)
    image_pre = pre_gradient(image_embed, image_scale, image_grad)
    text_pre = pre_gradient(text_embed, text_scale, text_grad)
    image_back = lax.dot_general(
        image_pre, image_head, (((1,), (1,)), ((), ())), preferred_element_type=jnp.float32
    )
    text_back = lax.dot_general(
        text_pre, text_head, (((1,), (1,)), ((), ())), preferred_element_type=jnp.float32
    )
    image_wgrad = lax.dot_general(
        image_rows, image_pre, (((0,), (0,)), ((), ())), preferred_element_type=jnp.float32
    )
    text_wgrad = lax.dot_general(
        text_rows, text_pre, (((0,), (0,)), ((), ())), preferred_element_type=jnp.float32
    )
    image_total, text_total = lax.psum((image_wgrad, text_wgrad), ("blk", "rep"))
    return (image_back[None], text_back[None], image_total, text_total)


def solution(mesh):
    return jax.shard_map(
        shards,
        mesh=mesh,
        in_specs=(
            P("rep", "blk", None),
            P("rep", "blk", None),
            P(),
            P(),
            P("rep", "blk"),
            P("rep", "blk"),
        ),
        out_specs=(P("rep", "blk", None), P("rep", "blk", None), P(), P()),
        check_vma=False,
    )
```

profile of v0, /device:TPU:1, one launch (start us, length us, event | category | flops | bytes accessed | tf_op | source)
XLA Modules:
  0.0 279.5 jit_solution(11065053901846281296)
XLA Ops:
  7.2 1.4 copy-done
  8.6 2.3 multiply_reduce_fusion.3
  10.9 1.1 multiply_convert_fusion.5
  12.0 2.4 multiply_reduce_fusion.2
  14.4 1.1 copy-done.1
  15.5 1.0 multiply_convert_fusion.4
  16.7 6.9 %all-gather.1 = bf16[4,1,512]{2,1,0:T(2,128)(2,1)S(1)} all-gather(bf16[1,1,512]{2,1,0:T(2,128)(2,1)S(1)} %reshape.27), channel_id=1, replica_groups=mesh['blk'=4,'rep'=8] {'blk'}, dimensions={0}, use_global_device_ids=true | all-gather | bytes 5120 | tf_op jit(solution)/shard_map/all_gather | solution.py:40
  23.6 7.0 %all-gather = bf16[4,1,512]{2,1,0:T(2,128)(2,1)S(1)} all-gather(bf16[1,1,512]{2,1,0:T(2,128)(2,1)S(1)} %reshape.25), channel_id=1, replica_groups=mesh['blk'=4,'rep'=8] {'blk'}, dimensions={0}, use_global_device_ids=true | all-gather | bytes 5120 | tf_op jit(solution)/shard_map/all_gather | solution.py:44
  30.7 27.3 %all-gather.7.cloned.1.call-done = bf16[2048,768]{1,0:T(8,128)(2,1)} async-done(((bf16[512,768]{1,0:T(8,128)(2,1)}), bf16[2048,768]{1,0:T(8,128)(2,1)}) %all-gather.7.cloned.1.call-update) | async-done | bytes 3145744 | tf_op jit(solution)/shard_map/all_gather | solution.py:39
  58.0 9.4 %multiply_reduce_fusion = (f32[512]{0:T(512)S(1)}, f32[512,768]{1,0:T(8,128)}) fusion(f32[512,768]{1,0:T(8,128)} %copy-done.1, f32[512]{0:T(512)S(1)} %add_rsqrt_fusion, bf16[512,768]{1,0:T(8,128)(2,1)} %multiply_convert_fusion.5, bf16[2048,768]{1,0:T(8,128)(2,1)} %all-gather.7.cloned.1.call-done, bf16[512,768]{1,0:T(8,128)(2,1)} %multiply_convert_fusion.4, ...), kind=kOutput, calls=%fused_computation.6 | convolution fusion | flops 3230268928 | bytes 7878656 | tf_op jit(solution)/shard_map/dot_general | solution.py:50
  67.4 2.6 multiply_convert_fusion.2
  70.0 0.9 copy-done.2
  70.8 2.2 convolution_bitcast_fusion.1
  73.1 31.2 %all-gather.5.cloned.1.call-done = bf16[2048,768]{1,0:T(8,128)(2,1)} async-done(((bf16[512,768]{1,0:T(8,128)(2,1)}), bf16[2048,768]{1,0:T(8,128)(2,1)}) %all-gather.5.cloned.1.call-update) | async-done | bytes 3145744 | tf_op jit(solution)/shard_map/all_gather | solution.py:43
  104.2 8.1 %multiply_reduce_fusion.1 = (f32[512]{0:T(512)S(1)}, f32[512,768]{1,0:T(8,128)}) fusion(f32[512,768]{1,0:T(8,128)S(1)} %get-tuple-element.17, f32[512]{0:T(512)S(1)} %add_rsqrt_fusion.1, bf16[512,768]{1,0:T(8,128)(2,1)} %multiply_convert_fusion.4, bf16[2048,768]{1,0:T(8,128)(2,1)} %all-gather.5.cloned.1.call-done, ...), kind=kOutput, calls=%fused_computation.9 | convolution fusion | flops 3230268928 | bytes 7878656 | tf_op jit(solution)/shard_map/dot_general | solution.py:48
  112.3 1.8 multiply_convert_fusion.3
  114.1 0.9 copy-done.4
  115.0 2.7 convolution_bitcast_fusion
  117.7 1.1 copy-done.3
  118.8 3.3 %convolution_bitcast_fusion.3 = f32[1,512,768]{2,1,0:T(8,128)} fusion(bf16[512,768]{1,0:T(8,128)(2,1)S(1)} %copy-done.3, bf16[768,768]{1,0:T(8,128)(2,1)} %param.9), kind=kOutput, calls=%fused_computation.13 | convolution fusion | flops 603979776 | bytes 3538944 | tf_op jit(solution)/shard_map/dot_general | solution.py:60
  122.1 2.4 convolution_bitcast_fusion.2
  124.5 141.9 %all-reduce.3.cloned.1.call-done = (f32[1024,768]{0,1:T(8,128)}, f32[768,768]{0,1:T(8,128)}) async-done(((f32[1024,768]{0,1:T(8,128)}, f32[768,768]{0,1:T(8,128)}), (f32[1024,768]{0,1:T(8,128)}, f32[768,768]{0,1:T(8,128)})) %all-reduce.3.cloned.1.call-update) | async-done | bytes 5505040 | tf_op jit(solution)/shard_map/psum | solution.py:69
  266.4 3.5 %copy.12 = f32[1024,768]{1,0:T(8,128)} copy(f32[1024,768]{0,1:T(8,128)} %get-tuple-element.12) | data formatting | bytes 6291456
  269.9 3.0 %copy.13 = f32[768,768]{1,0:T(8,128)} copy(f32[768,768]{0,1:T(8,128)} %get-tuple-element.13) | data formatting | bytes 4718592
  (29 shorter events, 0.3 us)
Async XLA Ops:
  7.2 1.4 copy-start
  7.2 50.8 %all-gather.7.cloned.1.call-start = ((), (), s32[]{:S(2)}) async-start(), calls=%async_computation.1 | async-start | bytes 3932160 | tf_op jit(solution)/shard_map/all_gather | solution.py:39
  12.0 92.3 %all-gather.5.cloned.1.call-start = ((), (), s32[]{:S(2)}) async-start(), calls=%async_computation | async-start | bytes 3932160 | tf_op jit(solution)/shard_map/all_gather | solution.py:43
  14.4 1.1 copy-start.1
  15.5 1.1 copy-start.9
  15.5 8.0 %copy-start.8 = (f32[1,512]{1,0:T(1,128)S(1)}, f32[1,512]{1,0:T(1,128)}, u32[]{:S(2)}) copy-start(f32[1,512]{1,0:T(1,128)} %param.11) | copy-start | bytes 6148
  16.6 249.8 %all-reduce.3.cloned.1.call-start = ((), (), s32[]{:S(2)}) async-start(), calls=%async_computation.2 | async-start | bytes 11010048 | tf_op jit(solution)/shard_map/psum | solution.py:69
  67.4 3.5 %copy-start.7 = (bf16[1,512,768]{2,1,0:T(8,128)(2,1)S(1)}, bf16[1,512,768]{2,1,0:T(8,128)(2,1)}, u32[]{:S(2)}) copy-start(bf16[1,512,768]{2,1,0:T(8,128)(2,1)} %param.7) | copy-start | bytes 2359300
  69.9 0.9 copy-start.2
  112.3 2.7 copy-start.6
  114.1 0.9 copy-start.4
  117.7 1.1 copy-start.3
  118.8 3.3 %copy-start.5 = (bf16[512,768]{1,0:T(8,128)(2,1)S(1)}, bf16[512,768]{1,0:T(8,128)(2,1)}, u32[]{:S(2)}) copy-start(bf16[512,768]{1,0:T(8,128)(2,1)} %copy-done.4) | copy-start | bytes 2359300
Sparse Core Ops, SparseCore 0:
  12.1 45.8 all-gather.6
  60.4 43.8 all-gather.4
  117.8 148.5 all-reduce.2
where the time goes:
time: 282 us; the launch traced here: 280 us
  waiting for transfers between devices  200 us (71%)
  matrix products  32.7 us (12%)
  blocking collectives  13.9 us (5%)
  between operations  13.9 us (5%)
  local copies, waits for them, and re-layouts  12 us (4%)
  other arithmetic  6.51 us (2%)
    psum x1, waiting for transfers between devices, shards(): lax.psum((image_wgrad, text_wgrad), ('blk', 'rep'))  142 us
    all_gather x1, waiting for transfers between devices, shards(): text_piece = lax.all_gather(text_round, 'blk', axis=0, tiled=True)  31.2 us
    all_gather x1, waiting for transfers between devices, shards(): image_piece = lax.all_gather(image_round, 'blk', axis=0, tiled=True)  27.3 us
    unnamed x24, local copies, waits for them, and re-layouts  12 us
    dot_general x1, matrix products, shards(): lax.dot_general(text_weights, image_piece, (((0,), (0,)), ((), ())), pref...  9.41 us
    dot_general x1, matrix products, shards(): jnp.dot(image_weights, text_piece, preferred_element_type=jnp.float32)  8.08 us
    all_gather x1, blocking collectives, shards(): lax.all_gather(lse_txt.astype(jnp.bfloat16), 'blk', axis=0, tiled=True)  7.04 us
    all_gather x1, blocking collectives, shards(): lax.all_gather(lse_img.astype(jnp.bfloat16), 'blk', axis=0, tiled=True)  6.89 us
  transfers between devices with their start and end apart: 3, of which 3 were waited for; matrix products, arithmetic and copies ran while one was open for 8% of the time, Pallas kernels for 0%

commit v1 on v0

--- a/solution.py
+++ b/solution.py
@@ -1,6 +1,10 @@
+import functools
+
 import jax
 import jax.numpy as jnp
 from jax import lax
+from jax.experimental import pallas as pl
+from jax.experimental.pallas import tpu as pltpu
 from jax.sharding import PartitionSpec as P
 
 logit_scale = 50.0
@@ -70,9 +74,291 @@
     return (image_back[None], text_back[None], image_total, text_total)
 
 
+MESH = pl.DeviceIdType.MESH
+SIDE = 2
+NT = (((1,), (1,)), ((), ()))
+TN = (((0,), (0,)), ((), ()))
+
+
+def mm(a, b, dims=(((1,), (0,)), ((), ()))):
+    return lax.dot_general(a, b, dims, preferred_element_type=jnp.float32)
+
+
+def fused(
+    nz, chunk,
+    xi, xt, wi, wt, li, lt,
+    pre_i, pre_t, hi, ht,
+    ei, et, fi, ft, im, ip, tm, tp, lip, ltp, u, v, w,
+    ps_i, pr_i, ps_t, pr_t, acc_i, acc_t, xit, xtt,
+    out_half, own, from_core, r1, r2, r3, full,
+    send, recv,
+):
+    n, e = im.shape
+    di, dt = wi.shape[0], wt.shape[0]
+    count = n // chunk
+    b, r = lax.axis_index("blk"), lax.axis_index("rep")
+    x, y = lax.rem(b, 2), b // 2
+    core, z = lax.rem(r, 2), r // 2
+    px = {"blk": y * 2 + 1 - x, "rep": r}
+    py = {"blk": (1 - y) * 2 + x, "rep": r}
+    pc = {"blk": b, "rep": z * 2 + 1 - core}
+    pz = [{"blk": b, "rep": lax.rem(z + k, nz) * 2 + core} for k in range(1, nz)]
+
+    used = [0]
+
+    def push(src, dst, dev):
+        s = used[0]
+        used[0] += 1
+        copy = pltpu.make_async_remote_copy(
+            src_ref=src, dst_ref=dst, send_sem=send.at[s], recv_sem=recv.at[s],
+            device_id=dev, device_id_type=MESH,
+        )
+        copy.start()
+        started.append(copy)
+        return copy
+
+    started = []
+    barrier = pltpu.get_barrier_semaphore()
+    for dev in [px, py, pc] + pz:
+        pl.semaphore_signal(barrier, inc=1, device_id=dev, device_id_type=MESH)
+
+    def project(c, feats, head, embed, factor, rounded):
+        rows = pl.ds(c * chunk, chunk)
+        raw = mm(feats[rows, :], head[...])
+        f = lax.rsqrt(jnp.sum(raw * raw, axis=1, keepdims=True) + epsilon)
+        out = raw * f
+        embed[rows, :] = out
+        factor[rows, :] = f
+        rounded[rows, :] = out.astype(jnp.bfloat16)
+
+    got_i, got_t = [], []
+    for c in range(count):
+        rows = pl.ds(c * chunk, chunk)
+        project(c, xi, wi, ei, fi, im)
+        if c == 0:
+            pl.semaphore_wait(barrier, 2 + nz)
+            got_li = push(li, lip, px)
+            got_lt = push(lt, ltp, py)
+        got_i.append(push(im.at[rows, :], ip.at[rows, :], px))
+        project(c, xt, wt, et, ft, tm)
+        got_t.append(push(tm.at[rows, :], tp.at[rows, :], py))
+
+    def columns(lse):
+        half = 0.5 * jnp.exp(-lse)
+        return jnp.transpose(jnp.broadcast_to(half, (128, n)))
+
+    u[0] = columns(li[...])
+    v[0] = 0.5 * jnp.exp(-lt[...])
+    images, texts = (im, ip), (tm, tp)
+
+    def tile(p, q, r0, nr, c0, nc):
+        s = logit_scale * mm(images[p][pl.ds(r0, nr), :], texts[q][pl.ds(c0, nc), :], NT)
+        fac = u[p, pl.ds(r0, nr), :][:, :1] + v[q, :, pl.ds(c0, nc)]
+        w[p, q, pl.ds(r0, nr), pl.ds(c0, nc)] = (jnp.exp(s) * fac).astype(jnp.bfloat16)
+
+    @pl.loop(0, count)
+    def _(c):
+        tile(0, 0, pl.multiple_of(c * chunk, chunk), chunk, 0, n)
+
+    @pl.loop(0, count)
+    def _(c):
+        rows = pl.ds(pl.multiple_of(c * chunk, chunk), chunk)
+        acc_i[rows, :] = mm(w[0, 0, rows, :], tm[...])
+        acc_t[rows, :] = mm(w[0, 0, :, rows], im[...], TN)
+
+    for src, dst, width in ((xi, xit, di), (xt, xtt, dt)):
+
+        @pl.loop(0, width // 128)
+        def _(k, src=src, dst=dst):
+            part = pl.ds(pl.multiple_of(k * 128, 128), 128)
+            dst[part, :] = jnp.transpose(src[:, part])
+
+    got_li.wait_recv()
+    got_lt.wait_recv()
+    u[1] = columns(lip[...])
+    v[1] = 0.5 * jnp.exp(-ltp[...])
+    for c in range(count):
+        got_i[c].wait_recv()
+        tile(1, 0, c * chunk, chunk, 0, n)
+        got_t[c].wait_recv()
+
+        tile(0, 1, 0, n, c * chunk, chunk)
+
+    sum_i, sum_t = [], []
+    for c in range(count):
+        rows = pl.ds(c * chunk, chunk)
+        tile(1, 1, c * chunk, chunk, 0, n)
+        ps_i[rows, :] = (mm(w[1, 0, rows, :], tm[...]) + mm(w[1, 1, rows, :], tp[...])).astype(
+            jnp.bfloat16
+        )
+        sum_i.append(push(ps_i.at[rows, :], pr_i.at[rows, :], px))
+    for c in range(count):
+        rows = pl.ds(c * chunk, chunk)
+        ps_t[rows, :] = (
+            mm(w[0, 1, :, rows], im[...], TN) + mm(w[1, 1, :, rows], ip[...], TN)
+        ).astype(jnp.bfloat16)
+        sum_t.append(push(ps_t.at[rows, :], pr_t.at[rows, :], py))
+
+    @pl.loop(0, count)
+    def _(c):
+        rows = pl.ds(pl.multiple_of(c * chunk, chunk), chunk)
+        acc_i[rows, :] += mm(w[0, 1, rows, :], tp[...])
+        acc_t[rows, :] += mm(w[1, 0, :, rows], ip[...], TN)
+
+    def finish(c, acc, part, other, embed, factor, out):
+        rows = pl.ds(c * chunk, chunk)
+        total = acc[rows, :] + part[rows, :].astype(jnp.float32)
+        grad = logit_scale * total - logit_scale * other[rows, :].astype(jnp.float32)
+        out[rows, :] = pre_gradient(embed[rows, :], factor[rows, :], grad)
+
+    for c in range(count):
+        sum_i[c].wait_recv()
+        finish(c, acc_i, pr_i, tm, ei, fi, pre_i)
+        sum_t[c].wait_recv()
+        finish(c, acc_t, pr_t, im, et, ft, pre_t)
+
+    eh = e // 2
+    bi, bt = di // (8 * nz), dt // (8 * nz)
+
+    def head_half(which, dst):
+        for q in range(4):
+            rows = pl.ds(pl.multiple_of(which * (di // 2) + q * nz * bi, nz * bi), nz * bi)
+            g = mm(xit[rows, :], pre_i[...]).astype(jnp.bfloat16)
+            for ab in range(2):
+                for k in range(nz):
+                    dst[ab, q // 2, q % 2, k, 0:bi, :] = g[k * bi : (k + 1) * bi, ab * eh : (ab + 1) * eh]
+            rows = pl.ds(pl.multiple_of(which * (dt // 2) + q * nz * bt, nz * bt), nz * bt)
+            g = mm(xtt[rows, :], pre_t[...])
+            for ab in range(2):
+                for k in range(nz):
+                    dst[ab, q // 2, q % 2, k, bi : bi + bt, :] = g[
+                        k * bt : (k + 1) * bt, ab * eh : (ab + 1) * eh
+                    ].astype(jnp.bfloat16)
+
+    def added(p, q):
+        return (p.astype(jnp.float32) + q.astype(jnp.float32)).astype(jnp.bfloat16)
+
+    ij = ((x, y), (y, x))
+    pi, pj = (px, py), (py, px)
+    head_half(1 - core, out_half)
+    first = [push(out_half.at[ab, 1 - ij[ab][0]], from_core.at[ab, 1 - ij[ab][0]], pc) for ab in range(2)]
+    second = [push(out_half.at[ab, ij[ab][0]], from_core.at[ab, ij[ab][0]], pc) for ab in range(2)]
+    head_half(core, own)
+    s1 = []
+    for ab in range(2):
+        i = ij[ab][0]
+        first[ab].wait_recv()
+        own[ab, 1 - i] = added(own[ab, 1 - i], from_core[ab, 1 - i])
+        s1.append(push(own.at[ab, 1 - i], r1.at[ab], pi[ab]))
+    for ab in range(2):
+        i = ij[ab][0]
+        second[ab].wait_recv()
+        own[ab, i] = added(own[ab, i], from_core[ab, i])
+    s2 = []
+    for ab in range(2):
+        i, j = ij[ab]
+        s1[ab].wait_recv()
+        own[ab, i] = added(own[ab, i], r1[ab])
+        s2.append(push(own.at[ab, i, 1 - j], r2.at[ab], pj[ab]))
+    s3 = []
+    for ab in range(2):
+        i, j = ij[ab]
+        s2[ab].wait_recv()
+        own[ab, i, j] = added(own[ab, i, j], r2[ab])
+        s3.append(
+            [push(own.at[ab, i, j, lax.rem(z + k, nz)], r3.at[ab, k], pz[k - 1]) for k in range(1, nz)]
+        )
+    s4 = []
+    for ab in range(2):
+        i, j = ij[ab]
+        total = own[ab, i, j, z].astype(jnp.float32)
+        for k in range(1, nz):
+            s3[ab][k - 1].wait_recv()
+            total = total + r3[ab, k].astype(jnp.float32)
+        full[core, ab, i, j, z] = total.astype(jnp.bfloat16)
+        piece = full.at[core, ab, i, j, z]
+        s4.append([push(piece, piece, pz[k - 1]) for k in range(1, nz)])
+    s5 = []
+    for ab in range(2):
+        i, j = ij[ab]
+        for copy in s4[ab]:
+            copy.wait_recv()
+        piece = full.at[core, ab, i, j]
+        s5.append(push(piece, piece, pj[ab]))
+    s6, last = [], []
+    for ab in range(2):
+        i, j = ij[ab]
+        s5[ab].wait_recv()
+        piece = full.at[core, ab, i]
+        s6.append(push(piece, piece, pi[ab]))
+        last.append(push(piece, piece, pc))
+    for ab in range(2):
+        i, j = ij[ab]
+        s6[ab].wait_recv()
+        piece = full.at[core, ab, 1 - i]
+        last.append(push(piece, piece, pc))
+    for copy in last:
+        copy.wait_recv()
+    for cc in range(2):
+        for ab in range(2):
+            for q in range(4):
+                for k in range(nz):
+                    p = q * nz + k
+                    cols = pl.ds(ab * eh, eh)
+                    piece = full[cc, ab, q // 2, q % 2, k]
+                    hi[pl.ds(cc * (di // 2) + p * bi, bi), cols] = piece[:bi]
+                    ht[pl.ds(cc * (dt // 2) + p * bt, bt), cols] = piece[bi:]
+    for copy in started:
+        copy.wait_send()
+
+
+def kernel_shards(nz, image_feats, text_feats, image_head, text_head, image_lse, text_lse):
+    n, di = image_feats.shape[1:]
+    dt, e = text_head.shape
+    chunk = n // 4
+    bf, f32 = jnp.bfloat16, jnp.float32
+    pr, eh = (di + dt) // (8 * nz), e // 2
+    vm = pltpu.VMEM
+    pieces = lambda *lead: vm((*lead, pr, eh), bf)
+    copies = 2 + 4 * (n // chunk) + 4 + 2 + 2 + 2 * (nz - 1) * 2 + 2 + 2 + 4
+    spec = pl.BlockSpec(memory_space=pltpu.VMEM)
+    pre_i, pre_t, hi, ht = pl.pallas_call(
+        functools.partial(fused, nz, chunk),
+        out_shape=[
+            jax.ShapeDtypeStruct((n, e), bf),
+            jax.ShapeDtypeStruct((n, e), bf),
+            jax.ShapeDtypeStruct((di, e), bf),
+            jax.ShapeDtypeStruct((dt, e), bf),
+        ],
+        in_specs=[spec] * 6,
+        out_specs=[spec] * 4,
+        scratch_shapes=[
+            vm((n, e), f32), vm((n, e), f32), vm((n, 1), f32), vm((n, 1), f32),
+            vm((n, e), bf), vm((n, e), bf), vm((n, e), bf), vm((n, e), bf),
+            vm((1, n), f32), vm((1, n), f32), vm((2, n, 128), f32), vm((2, 1, n), f32),
+            vm((2, 2, n, n), bf),
+            vm((n, e), bf), vm((n, e), bf), vm((n, e), bf), vm((n, e), bf),
+            vm((n, e), f32), vm((n, e), f32), vm((di, n), bf), vm((dt, n), bf),
+            pieces(2, 2, 2, nz), pieces(2, 2, 2, nz), pieces(2, 2, 2, nz),
+            pieces(2, 2, nz), pieces(2, nz), pieces(2, nz), pieces(2, 2, 2, 2, nz),
+            pltpu.SemaphoreType.DMA((copies,)), pltpu.SemaphoreType.DMA((copies,)),
+        ],
+        compiler_params=pltpu.CompilerParams(
+            collective_id=0, has_side_effects=True, vmem_limit_bytes=60 * 1024 * 1024
+        ),
+    )(image_feats[0], text_feats[0], image_head, text_head, image_lse, text_lse)
+    image_back = lax.dot_general(pre_i, image_head, NT, preferred_element_type=f32)
+    text_back = lax.dot_general(pre_t, text_head, NT, preferred_element_type=f32)
+    return (image_back[None], text_back[None], hi.astype(f32), ht.astype(f32))
+
+
 def solution(mesh):
+    blk, rep = mesh.shape["blk"], mesh.shape["rep"]
+    body = shards
+    if blk == SIDE * SIDE and rep % SIDE == 0:
+        body = functools.partial(kernel_shards, rep // SIDE)
     return jax.shard_map(
-        shards,
+        body,
         mesh=mesh,
         in_specs=(
             P("rep", "blk", None),

time: 282 us -> 110 us (0.39)
  waiting for transfers between devices: 200 us -> 0 us
  Pallas kernels: 0 us -> 99.3 us
  matrix products: 32.7 us -> 4.29 us
  blocking collectives: 13.9 us -> 0 us
  between operations: 13.9 us -> 0.65 us
  local copies, waits for them, and re-layouts: 12 us -> 0.89 us
    psum x1 -> x0, waiting for transfers between devices: 142 us -> none  [shards(): lax.psum((image_wgrad, text_wgrad), ('blk', 'rep'))]
    pallas_call x0 -> x1, Pallas kernels: none -> 99.3 us  [kernel_shards(): pl.pallas_call(functools.partial(fused, nz, chunk), out_shape=[jax.ShapeD...]
    all_gather x2 -> x0, waiting for transfers between devices: 58.5 us -> none  [the longest x1 31.2 us: shards(): text_piece = lax.all_gather(text_round, 'blk', axis=0, tiled=True)]
    dot_general x8 -> x2, matrix products: 32.7 us -> 4.29 us  [the longest x1 2.33 us: kernel_shards(): lax.dot_general(pre_i, image_head, NT, preferred_element_type=f32)]
    all_gather x2 -> x0, blocking collectives: 13.9 us -> none  [the longest x1 7.04 us: shards(): lax.all_gather(lse_txt.astype(jnp.bfloat16), 'blk', axis=0, tiled=True)]
    unnamed x24 -> x10, local copies, waits for them, and re-layouts: 12 us -> 0.89 us
    convert_element_type x8 -> x2, other arithmetic: 6.49 us -> 4.98 us  [kernel_shards(): return (image_back[None], text_back[None], hi.astype(f32), ht.astype(f32))]
  transfers between devices with their start and end apart: 3 -> 0, of which waited for: 3 -> 0; matrix products, arithmetic and copies ran while one was open for 8% -> 0% of each run, Pallas kernels for 0% -> 0%
where the time goes in v1:
time: 110 us
  Pallas kernels  99.3 us (90%)
  other arithmetic  4.98 us (5%)
  matrix products  4.29 us (4%)
    pallas_call x1, Pallas kernels, kernel_shards(): pl.pallas_call(functools.partial(fused, nz, chunk), out_shape=[jax.ShapeD...  99.3 us
    convert_element_type x2, other arithmetic, kernel_shards(): return (image_back[None], text_back[None], hi.astype(f32), ht.astype(f32))  4.98 us
    dot_general x1, matrix products, kernel_shards(): lax.dot_general(pre_i, image_head, NT, preferred_element_type=f32)  2.33 us

profile of v1, /device:TPU:1, one launch (start us, length us, event | category | flops | bytes accessed | tf_op | source)
XLA Modules:
  0.0 110.1 jit_solution(12145107593028948626)
XLA Ops:
  0.6 99.3 %shard_map.93 = (bf16[512,768]{1,0:T(8,128)(2,1)}, bf16[512,768]{1,0:T(8,128)(2,1)}, bf16[1024,768]{1,0:T(8,128)(2,1)}, bf16[768,768]{1,0:T(8,128)(2,1)}) custom-call(bf16[512,1024]{1,0:T(8,128)(2,1)} %bitcast.10, bf16[512,768]{1,0:T(8,128)(2,1)} %bitcast.11, bf16[1024,768]{1,0:T(8,128)(2,1)} %wi.1, bf16[768,768]{1,0:T(8,128)(2,1)} %wt.1, f32[1,512]{1,0:T(1,128)} %li.1, ...), custom_call_target="tpu_custom_call" | custom-call | tf_op jit(solution)/shard_map/pallas_call | solution.py:325
  100.0 0.0 copy-start.1
  100.0 3.4 %convert_element_type.6 = f32[1024,768]{1,0:T(8,128)} convert(bf16[1024,768]{1,0:T(8,128)(2,1)} %get-tuple-element.10) | non-fusion elementwise | flops 786432 | bytes 4718592 | tf_op jit(solution)/shard_map/convert_element_type | solution.py:352
  103.4 0.0 copy-done.1
  103.4 0.0 copy-start
  103.4 0.0 copy-start.4
  103.4 1.6 %convert_element_type.7 = f32[768,768]{1,0:T(8,128)} convert(bf16[768,768]{1,0:T(8,128)(2,1)S(1)} %copy-done.1) | non-fusion elementwise | flops 589824 | bytes 3538944 | tf_op jit(solution)/shard_map/convert_element_type | solution.py:352
  104.9 0.5 copy-done
  105.5 0.3 copy-done.4
  105.8 0.0 copy-start.2
  105.8 0.0 copy-start.3
  105.8 2.3 %convolution_bitcast_fusion = f32[1,512,1024]{2,1,0:T(8,128)} fusion(bf16[512,768]{1,0:T(8,128)(2,1)S(1)} %copy-done.4, bf16[1024,768]{1,0:T(8,128)(2,1)S(1)} %copy-done), kind=kOutput, calls=%fused_computation | convolution fusion | flops 805306368 | bytes 4456448 | tf_op jit(solution)/shard_map/dot_general | solution.py:350
  108.2 0.0 copy-done.2
  108.2 0.0 copy-done.3
  108.2 2.0 %convolution_bitcast_fusion.1 = f32[1,512,768]{2,1,0:T(8,128)} fusion(bf16[512,768]{1,0:T(8,128)(2,1)S(1)} %copy-done.3, bf16[768,768]{1,0:T(8,128)(2,1)S(1)} %copy-done.2), kind=kOutput, calls=%fused_computation.1 | convolution fusion | flops 603979776 | bytes 3538944 | tf_op jit(solution)/shard_map/dot_general | solution.py:351
Async XLA Ops:
  100.0 3.4 %copy-start.1 = (bf16[768,768]{1,0:T(8,128)(2,1)S(1)}, bf16[768,768]{1,0:T(8,128)(2,1)}, u32[]{:S(2)}) copy-start(bf16[768,768]{1,0:T(8,128)(2,1)} %get-tuple-element.11) | copy-start | bytes 3538948
  103.4 2.1 %copy-start = (bf16[1024,768]{1,0:T(8,128)(2,1)S(1)}, bf16[1024,768]{1,0:T(8,128)(2,1)}, u32[]{:S(2)}) copy-start(bf16[1024,768]{1,0:T(8,128)(2,1)} %wi.1) | copy-start | bytes 4718596
  103.4 2.5 %copy-start.4 = (bf16[512,768]{1,0:T(8,128)(2,1)S(1)}, bf16[512,768]{1,0:T(8,128)(2,1)}, u32[]{:S(2)}) copy-start(bf16[512,768]{1,0:T(8,128)(2,1)} %get-tuple-element.8) | copy-start | bytes 2359300
  105.8 2.3 %copy-start.2 = (bf16[768,768]{1,0:T(8,128)(2,1)S(1)}, bf16[768,768]{1,0:T(8,128)(2,1)}, u32[]{:S(2)}) copy-start(bf16[768,768]{1,0:T(8,128)(2,1)} %wt.1) | copy-start | bytes 3538948
  105.8 2.3 %copy-start.3 = (bf16[512,768]{1,0:T(8,128)(2,1)S(1)}, bf16[512,768]{1,0:T(8,128)(2,1)}, u32[]{:S(2)}) copy-start(bf16[512,768]{1,0:T(8,128)(2,1)} %get-tuple-element.9) | copy-start | bytes 2359300

commit v2 on v1

--- a/solution.py
+++ b/solution.py
@@ -90,7 +90,7 @@
     pre_i, pre_t, hi, ht,
     ei, et, fi, ft, im, ip, tm, tp, lip, ltp, u, v, w,
     ps_i, pr_i, ps_t, pr_t, acc_i, acc_t, xit, xtt,
-    out_half, own, from_core, r1, r2, r3, full,
+    bufs_i, bufs_t,
     send, recv,
 ):
     n, e = im.shape
@@ -183,17 +183,17 @@
         got_t[c].wait_recv()
 
         tile(0, 1, 0, n, c * chunk, chunk)
+        tile(1, 1, c * chunk, chunk, 0, (c + 1) * chunk)
+        if c > 0:
+            tile(1, 1, 0, c * chunk, c * chunk, chunk)
 
     sum_i, sum_t = [], []
     for c in range(count):
         rows = pl.ds(c * chunk, chunk)
-        tile(1, 1, c * chunk, chunk, 0, n)
         ps_i[rows, :] = (mm(w[1, 0, rows, :], tm[...]) + mm(w[1, 1, rows, :], tp[...])).astype(
             jnp.bfloat16
         )
         sum_i.append(push(ps_i.at[rows, :], pr_i.at[rows, :], px))
-    for c in range(count):
-        rows = pl.ds(c * chunk, chunk)
         ps_t[rows, :] = (
             mm(w[0, 1, :, rows], im[...], TN) + mm(w[1, 1, :, rows], ip[...], TN)
         ).astype(jnp.bfloat16)
@@ -218,96 +218,111 @@
         finish(c, acc_t, pr_t, im, et, ft, pre_t)
 
     eh = e // 2
-    bi, bt = di // (8 * nz), dt // (8 * nz)
-
-    def head_half(which, dst):
-        for q in range(4):
-            rows = pl.ds(pl.multiple_of(which * (di // 2) + q * nz * bi, nz * bi), nz * bi)
-            g = mm(xit[rows, :], pre_i[...]).astype(jnp.bfloat16)
-            for ab in range(2):
-                for k in range(nz):
-                    dst[ab, q // 2, q % 2, k, 0:bi, :] = g[k * bi : (k + 1) * bi, ab * eh : (ab + 1) * eh]
-            rows = pl.ds(pl.multiple_of(which * (dt // 2) + q * nz * bt, nz * bt), nz * bt)
-            g = mm(xtt[rows, :], pre_t[...])
-            for ab in range(2):
-                for k in range(nz):
-                    dst[ab, q // 2, q % 2, k, bi : bi + bt, :] = g[
-                        k * bt : (k + 1) * bt, ab * eh : (ab + 1) * eh
-                    ].astype(jnp.bfloat16)
 
     def added(p, q):
         return (p.astype(jnp.float32) + q.astype(jnp.float32)).astype(jnp.bfloat16)
 
     ij = ((x, y), (y, x))
     pi, pj = (px, py), (py, px)
-    head_half(1 - core, out_half)
-    first = [push(out_half.at[ab, 1 - ij[ab][0]], from_core.at[ab, 1 - ij[ab][0]], pc) for ab in range(2)]
-    second = [push(out_half.at[ab, ij[ab][0]], from_core.at[ab, ij[ab][0]], pc) for ab in range(2)]
-    head_half(core, own)
-    s1 = []
-    for ab in range(2):
-        i = ij[ab][0]
-        first[ab].wait_recv()
-        own[ab, 1 - i] = added(own[ab, 1 - i], from_core[ab, 1 - i])
-        s1.append(push(own.at[ab, 1 - i], r1.at[ab], pi[ab]))
-    for ab in range(2):
-        i = ij[ab][0]
-        second[ab].wait_recv()
-        own[ab, i] = added(own[ab, i], from_core[ab, i])
-    s2 = []
-    for ab in range(2):
-        i, j = ij[ab]
-        s1[ab].wait_recv()
-        own[ab, i] = added(own[ab, i], r1[ab])
-        s2.append(push(own.at[ab, i, 1 - j], r2.at[ab], pj[ab]))
-    s3 = []
-    for ab in range(2):
-        i, j = ij[ab]
-        s2[ab].wait_recv()
-        own[ab, i, j] = added(own[ab, i, j], r2[ab])
-        s3.append(
-            [push(own.at[ab, i, j, lax.rem(z + k, nz)], r3.at[ab, k], pz[k - 1]) for k in range(1, nz)]
-        )
-    s4 = []
-    for ab in range(2):
-        i, j = ij[ab]
-        total = own[ab, i, j, z].astype(jnp.float32)
-        for k in range(1, nz):
-            s3[ab][k - 1].wait_recv()
-            total = total + r3[ab, k].astype(jnp.float32)
-        full[core, ab, i, j, z] = total.astype(jnp.bfloat16)
-        piece = full.at[core, ab, i, j, z]
-        s4.append([push(piece, piece, pz[k - 1]) for k in range(1, nz)])
-    s5 = []
-    for ab in range(2):
-        i, j = ij[ab]
-        for copy in s4[ab]:
+    both = range(2)
+
+    def head_half(which, dst, flipped, pre):
+        part = dst.shape[4]
+        half = flipped.shape[0] // 2
+        for q in range(4):
+            rows = pl.ds(pl.multiple_of(which * half + q * nz * part, nz * part), nz * part)
+            g = mm(flipped[rows, :], pre[...])
+            for ab in both:
+                for k in range(nz):
+                    dst[ab, q // 2, q % 2, k] = g[
+                        k * part : (k + 1) * part, ab * eh : (ab + 1) * eh
+                    ].astype(jnp.bfloat16)
+
+    def reduce_head(flipped, pre, result, out_half, own, from_core, r1, r2, r3, full):
+        head_half(1 - core, out_half, flipped, pre)
+        first, second = [
+            [push(out_half.at[ab, i], from_core.at[ab, i], pc) for ab, i in places]
+            for places in (
+                [(ab, 1 - ij[ab][0]) for ab in both],
+                [(ab, ij[ab][0]) for ab in both],
+            )
+        ]
+        head_half(core, own, flipped, pre)
+        s1 = []
+        for ab in both:
+            i = ij[ab][0]
+            first[ab].wait_recv()
+            own[ab, 1 - i] = added(own[ab, 1 - i], from_core[ab, 1 - i])
+            s1.append(push(own.at[ab, 1 - i], r1.at[ab], pi[ab]))
+        for ab in both:
+            i = ij[ab][0]
+            second[ab].wait_recv()
+            own[ab, i] = added(own[ab, i], from_core[ab, i])
+        yield
+        s2 = []
+        for ab in both:
+            i, j = ij[ab]
+            s1[ab].wait_recv()
+            own[ab, i] = added(own[ab, i], r1[ab])
+            s2.append(push(own.at[ab, i, 1 - j], r2.at[ab], pj[ab]))
+        yield
+        s3 = []
+        for ab in both:
+            i, j = ij[ab]
+            s2[ab].wait_recv()
+            own[ab, i, j] = added(own[ab, i, j], r2[ab])
+            s3.append(
+                [push(own.at[ab, i, j, lax.rem(z + k, nz)], r3.at[ab, k], pz[k - 1]) for k in range(1, nz)]
+            )
+        yield
+        s4 = []
+        for ab in both:
+            i, j = ij[ab]
+            total = own[ab, i, j, z].astype(jnp.float32)
+            for k in range(1, nz):
+                s3[ab][k - 1].wait_recv()
+                total = total + r3[ab, k].astype(jnp.float32)
+            full[core, ab, i, j, z] = total.astype(jnp.bfloat16)
+            piece = full.at[core, ab, i, j, z]
+            s4.append([push(piece, piece, pz[k - 1]) for k in range(1, nz)])
+        yield
+        s5 = []
+        for ab in both:
+            i, j = ij[ab]
+            for copy in s4[ab]:
+                copy.wait_recv()
+            piece = full.at[core, ab, i, j]
+            s5.append(push(piece, piece, pj[ab]))
+        yield
+        s6, last = [], []
+        for ab in both:
+            i, j = ij[ab]
+            s5[ab].wait_recv()
+            piece = full.at[core, ab, i]
+            s6.append(push(piece, piece, pi[ab]))
+            last.append(push(piece, piece, pc))
+        yield
+        for ab in both:
+            i, j = ij[ab]
+            s6[ab].wait_recv()
+            piece = full.at[core, ab, 1 - i]
+            last.append(push(piece, piece, pc))
+        for copy in last:
             copy.wait_recv()
-        piece = full.at[core, ab, i, j]
-        s5.append(push(piece, piece, pj[ab]))
-    s6, last = [], []
-    for ab in range(2):
-        i, j = ij[ab]
-        s5[ab].wait_recv()
-        piece = full.at[core, ab, i]
-        s6.append(push(piece, piece, pi[ab]))
-        last.append(push(piece, piece, pc))
-    for ab in range(2):
-        i, j = ij[ab]
-        s6[ab].wait_recv()
-        piece = full.at[core, ab, 1 - i]
-        last.append(push(piece, piece, pc))
-    for copy in last:
-        copy.wait_recv()
-    for cc in range(2):
-        for ab in range(2):
-            for q in range(4):
-                for k in range(nz):
-                    p = q * nz + k
-                    cols = pl.ds(ab * eh, eh)
-                    piece = full[cc, ab, q // 2, q % 2, k]
-                    hi[pl.ds(cc * (di // 2) + p * bi, bi), cols] = piece[:bi]
-                    ht[pl.ds(cc * (dt // 2) + p * bt, bt), cols] = piece[bi:]
+        part = full.shape[5]
+        for cc in both:
+            for ab in both:
+                for q in range(4):
+                    for k in range(nz):
+                        result[
+                            pl.ds(((cc * 4 + q) * nz + k) * part, part), pl.ds(ab * eh, eh)
+                        ] = full[cc, ab, q // 2, q % 2, k]
+        yield
+
+    parts = [reduce_head(xtt, pre_t, ht, *bufs_t), reduce_head(xit, pre_i, hi, *bufs_i)]
+    for _ in range(7):
+        for step in parts:
+            next(step)
     for copy in started:
         copy.wait_send()
 
@@ -317,10 +332,13 @@
     dt, e = text_head.shape
     chunk = n // 4
     bf, f32 = jnp.bfloat16, jnp.float32
-    pr, eh = (di + dt) // (8 * nz), e // 2
     vm = pltpu.VMEM
-    pieces = lambda *lead: vm((*lead, pr, eh), bf)
-    copies = 2 + 4 * (n // chunk) + 4 + 2 + 2 + 2 * (nz - 1) * 2 + 2 + 2 + 4
+
+    def buffers(rows):
+        leads = [(2, 2, 2, nz)] * 3 + [(2, 2, nz), (2, nz), (2, nz), (2, 2, 2, 2, nz)]
+        return [vm((*lead, rows // (8 * nz), e // 2), bf) for lead in leads]
+
+    copies = 2 + 4 * (n // chunk) + 2 * (4 + 2 + 2 + 2 * (nz - 1) * 2 + 2 + 2 + 4)
     spec = pl.BlockSpec(memory_space=pltpu.VMEM)
     pre_i, pre_t, hi, ht = pl.pallas_call(
         functools.partial(fused, nz, chunk),
@@ -339,8 +357,7 @@
             vm((2, 2, n, n), bf),
             vm((n, e), bf), vm((n, e), bf), vm((n, e), bf), vm((n, e), bf),
             vm((n, e), f32), vm((n, e), f32), vm((di, n), bf), vm((dt, n), bf),
-            pieces(2, 2, 2, nz), pieces(2, 2, 2, nz), pieces(2, 2, 2, nz),
-            pieces(2, 2, nz), pieces(2, nz), pieces(2, nz), pieces(2, 2, 2, 2, nz),
+            buffers(di), buffers(dt),
             pltpu.SemaphoreType.DMA((copies,)), pltpu.SemaphoreType.DMA((copies,)),
         ],
         compiler_params=pltpu.CompilerParams(

time: 110 us -> 102 us (0.927)
  Pallas kernels: 99.3 us -> 91.2 us
    pallas_call x1, Pallas kernels: 99.3 us -> 91.2 us  [kernel_shards(): pl.pallas_call(functools.partial(fused, nz, chunk), out_shape=[jax.ShapeD...]
where the time goes in v2:
time: 102 us
  Pallas kernels  91.2 us (89%)
  other arithmetic  4.98 us (5%)
  matrix products  4.29 us (4%)
    pallas_call x1, Pallas kernels, kernel_shards(): pl.pallas_call(functools.partial(fused, nz, chunk), out_shape=[jax.ShapeD...  91.2 us
    convert_element_type x2, other arithmetic, kernel_shards(): return (image_back[None], text_back[None], hi.astype(f32), ht.astype(f32))  4.98 us
    dot_general x1, matrix products, kernel_shards(): lax.dot_general(pre_i, image_head, NT, preferred_element_type=f32)  2.33 us

profile of v2, /device:TPU:1, one launch (start us, length us, event | category | flops | bytes accessed | tf_op | source)
XLA Modules:
  0.0 102.0 jit_solution(7126126534069292168)
XLA Ops:
  0.6 91.2 %shard_map.93 = (bf16[512,768]{1,0:T(8,128)(2,1)}, bf16[512,768]{1,0:T(8,128)(2,1)}, bf16[1024,768]{1,0:T(8,128)(2,1)}, bf16[768,768]{1,0:T(8,128)(2,1)}) custom-call(bf16[512,1024]{1,0:T(8,128)(2,1)} %bitcast.10, bf16[512,768]{1,0:T(8,128)(2,1)} %bitcast.11, bf16[1024,768]{1,0:T(8,128)(2,1)} %wi.1, bf16[768,768]{1,0:T(8,128)(2,1)} %wt.1, f32[1,512]{1,0:T(1,128)} %li.1, ...), custom_call_target="tpu_custom_call" | custom-call | tf_op jit(solution)/shard_map/pallas_call | solution.py:343
  91.9 0.0 copy-start.1
  91.9 3.4 %convert_element_type.6 = f32[1024,768]{1,0:T(8,128)} convert(bf16[1024,768]{1,0:T(8,128)(2,1)} %get-tuple-element.10) | non-fusion elementwise | flops 786432 | bytes 4718592 | tf_op jit(solution)/shard_map/convert_element_type | solution.py:369
  95.3 0.0 copy-done.1
  95.3 0.0 copy-start
  95.3 0.0 copy-start.4
  95.3 1.6 %convert_element_type.7 = f32[768,768]{1,0:T(8,128)} convert(bf16[768,768]{1,0:T(8,128)(2,1)S(1)} %copy-done.1) | non-fusion elementwise | flops 589824 | bytes 3538944 | tf_op jit(solution)/shard_map/convert_element_type | solution.py:369
  96.8 0.5 copy-done
  97.4 0.3 copy-done.4
  97.7 0.0 copy-start.2
  97.7 0.0 copy-start.3
  97.7 2.3 %convolution_bitcast_fusion = f32[1,512,1024]{2,1,0:T(8,128)} fusion(bf16[512,768]{1,0:T(8,128)(2,1)S(1)} %copy-done.4, bf16[1024,768]{1,0:T(8,128)(2,1)S(1)} %copy-done), kind=kOutput, calls=%fused_computation | convolution fusion | flops 805306368 | bytes 4456448 | tf_op jit(solution)/shard_map/dot_general | solution.py:367
  100.1 0.0 copy-done.2
  100.1 0.0 copy-done.3
  100.1 2.0 %convolution_bitcast_fusion.1 = f32[1,512,768]{2,1,0:T(8,128)} fusion(bf16[512,768]{1,0:T(8,128)(2,1)S(1)} %copy-done.3, bf16[768,768]{1,0:T(8,128)(2,1)S(1)} %copy-done.2), kind=kOutput, calls=%fused_computation.1 | convolution fusion | flops 603979776 | bytes 3538944 | tf_op jit(solution)/shard_map/dot_general | solution.py:368
Async XLA Ops:
  91.9 3.4 %copy-start.1 = (bf16[768,768]{1,0:T(8,128)(2,1)S(1)}, bf16[768,768]{1,0:T(8,128)(2,1)}, u32[]{:S(2)}) copy-start(bf16[768,768]{1,0:T(8,128)(2,1)} %get-tuple-element.11) | copy-start | bytes 3538948
  95.3 2.1 %copy-start = (bf16[1024,768]{1,0:T(8,128)(2,1)S(1)}, bf16[1024,768]{1,0:T(8,128)(2,1)}, u32[]{:S(2)}) copy-start(bf16[1024,768]{1,0:T(8,128)(2,1)} %wi.1) | copy-start | bytes 4718596
  95.3 2.5 %copy-start.4 = (bf16[512,768]{1,0:T(8,128)(2,1)S(1)}, bf16[512,768]{1,0:T(8,128)(2,1)}, u32[]{:S(2)}) copy-start(bf16[512,768]{1,0:T(8,128)(2,1)} %get-tuple-element.8) | copy-start | bytes 2359300
  97.7 2.3 %copy-start.2 = (bf16[768,768]{1,0:T(8,128)(2,1)S(1)}, bf16[768,768]{1,0:T(8,128)(2,1)}, u32[]{:S(2)}) copy-start(bf16[768,768]{1,0:T(8,128)(2,1)} %wt.1) | copy-start | bytes 3538948
  97.7 2.3 %copy-start.3 = (bf16[512,768]{1,0:T(8,128)(2,1)S(1)}, bf16[512,768]{1,0:T(8,128)(2,1)}, u32[]{:S(2)}) copy-start(bf16[512,768]{1,0:T(8,128)(2,1)} %get-tuple-element.9) | copy-start | bytes 2359300

commit v3 on v2

--- a/solution.py
+++ b/solution.py
@@ -86,12 +86,13 @@
 
 def fused(
     nz, chunk,
-    xi, xt, wi, wt, li, lt,
-    pre_i, pre_t, hi, ht,
+    xi_in, xt_in, wi_in, wt_in, li, lt,
+    pre_i_out, pre_t_out, hi_out, ht_out,
+    xi, xt, wi, wt, pre_i, pre_t, hi, ht,
     ei, et, fi, ft, im, ip, tm, tp, lip, ltp, u, v, w,
     ps_i, pr_i, ps_t, pr_t, acc_i, acc_t, xit, xtt,
-    bufs_i, bufs_t,
-    send, recv,
+    bufs_low, bufs_high, bufs_t,
+    send, recv, local,
 ):
     n, e = im.shape
     di, dt = wi.shape[0], wt.shape[0]
@@ -117,7 +118,25 @@
         started.append(copy)
         return copy
 
-    started = []
+    started, moved = [], []
+
+    def move(src, dst):
+        copy = pltpu.make_async_copy(src, dst, local.at[len(moved)])
+        copy.start()
+        moved.append(copy)
+        return copy
+
+    def piece_of(c, feats_in, feats):
+        rows = pl.ds(c * chunk, chunk)
+        return move(feats_in.at[rows, :], feats.at[rows, :])
+
+    in_wi = move(wi_in, wi)
+    in_xi = [piece_of(0, xi_in, xi)]
+    in_wt = move(wt_in, wt)
+    in_xt = [piece_of(0, xt_in, xt)]
+    for c in range(1, count):
+        in_xi.append(piece_of(c, xi_in, xi))
+        in_xt.append(piece_of(c, xt_in, xt))
     barrier = pltpu.get_barrier_semaphore()
     for dev in [px, py, pc] + pz:
         pl.semaphore_signal(barrier, inc=1, device_id=dev, device_id_type=MESH)
@@ -134,12 +153,18 @@
     got_i, got_t = [], []
     for c in range(count):
         rows = pl.ds(c * chunk, chunk)
+        if c == 0:
+            in_wi.wait()
+        in_xi[c].wait()
         project(c, xi, wi, ei, fi, im)
         if c == 0:
             pl.semaphore_wait(barrier, 2 + nz)
             got_li = push(li, lip, px)
             got_lt = push(lt, ltp, py)
         got_i.append(push(im.at[rows, :], ip.at[rows, :], px))
+        if c == 0:
+            in_wt.wait()
+        in_xt[c].wait()
         project(c, xt, wt, et, ft, tm)
         got_t.append(push(tm.at[rows, :], tp.at[rows, :], py))
 
@@ -217,6 +242,7 @@
         sum_t[c].wait_recv()
         finish(c, acc_t, pr_t, im, et, ft, pre_t)
 
+    outputs = [move(pre_i, pre_i_out), move(pre_t, pre_t_out)]
     eh = e // 2
 
     def added(p, q):
@@ -238,7 +264,7 @@
                         k * part : (k + 1) * part, ab * eh : (ab + 1) * eh
                     ].astype(jnp.bfloat16)
 
-    def reduce_head(flipped, pre, result, out_half, own, from_core, r1, r2, r3, full):
+    def reduce_head(flipped, pre, result, result_out, out_half, own, from_core, r1, r2, r3, full):
         head_half(1 - core, out_half, flipped, pre)
         first, second = [
             [push(out_half.at[ab, i], from_core.at[ab, i], pc) for ab, i in places]
@@ -317,12 +343,20 @@
                         result[
                             pl.ds(((cc * 4 + q) * nz + k) * part, part), pl.ds(ab * eh, eh)
                         ] = full[cc, ab, q // 2, q % 2, k]
-        yield
-
-    parts = [reduce_head(xtt, pre_t, ht, *bufs_t), reduce_head(xit, pre_i, hi, *bufs_i)]
+        outputs.append(move(result, result_out))
+        yield
+
+    low, high = pl.ds(0, di // 2), pl.ds(di // 2, di // 2)
+    parts = [
+        reduce_head(xit.at[low, :], pre_i, hi.at[low, :], hi_out.at[low, :], *bufs_low),
+        reduce_head(xit.at[high, :], pre_i, hi.at[high, :], hi_out.at[high, :], *bufs_high),
+        reduce_head(xtt, pre_t, ht, ht_out, *bufs_t),
+    ]
     for _ in range(7):
         for step in parts:
             next(step)
+    for copy in outputs:
+        copy.wait()
     for copy in started:
         copy.wait_send()
 
@@ -338,8 +372,9 @@
         leads = [(2, 2, 2, nz)] * 3 + [(2, 2, nz), (2, nz), (2, nz), (2, 2, 2, 2, nz)]
         return [vm((*lead, rows // (8 * nz), e // 2), bf) for lead in leads]
 
-    copies = 2 + 4 * (n // chunk) + 2 * (4 + 2 + 2 + 2 * (nz - 1) * 2 + 2 + 2 + 4)
+    copies = 2 + 4 * (n // chunk) + 3 * (4 + 2 + 2 + 2 * (nz - 1) * 2 + 2 + 2 + 4)
     spec = pl.BlockSpec(memory_space=pltpu.VMEM)
+    anywhere = pl.BlockSpec(memory_space=pl.ANY)
     pre_i, pre_t, hi, ht = pl.pallas_call(
         functools.partial(fused, nz, chunk),
         out_shape=[
@@ -348,17 +383,20 @@
             jax.ShapeDtypeStruct((di, e), bf),
             jax.ShapeDtypeStruct((dt, e), bf),
         ],
-        in_specs=[spec] * 6,
-        out_specs=[spec] * 4,
+        in_specs=[anywhere] * 4 + [spec] * 2,
+        out_specs=[anywhere] * 4,
         scratch_shapes=[
+            vm((n, di), bf), vm((n, dt), bf), vm((di, e), bf), vm((dt, e), bf),
+            vm((n, e), bf), vm((n, e), bf), vm((di, e), bf), vm((dt, e), bf),
             vm((n, e), f32), vm((n, e), f32), vm((n, 1), f32), vm((n, 1), f32),
             vm((n, e), bf), vm((n, e), bf), vm((n, e), bf), vm((n, e), bf),
             vm((1, n), f32), vm((1, n), f32), vm((2, n, 128), f32), vm((2, 1, n), f32),
             vm((2, 2, n, n), bf),
             vm((n, e), bf), vm((n, e), bf), vm((n, e), bf), vm((n, e), bf),
             vm((n, e), f32), vm((n, e), f32), vm((di, n), bf), vm((dt, n), bf),
-            buffers(di), buffers(dt),
+            buffers(di // 2), buffers(di // 2), buffers(dt),
             pltpu.SemaphoreType.DMA((copies,)), pltpu.SemaphoreType.DMA((copies,)),
+            pltpu.SemaphoreType.DMA((2 + 2 * (n // chunk) + 5,)),
         ],
         compiler_params=pltpu.CompilerParams(
             collective_id=0, has_side_effects=True, vmem_limit_bytes=60 * 1024 * 1024

time: 102 us -> 101 us (level)
  Pallas kernels: 91.2 us -> 89.7 us
    pallas_call x1, Pallas kernels: 91.2 us -> 89.7 us  [kernel_shards(): pl.pallas_call(functools.partial(fused, nz, chunk), out_shape=[jax.ShapeD...]
where the time goes in v3:
time: 101 us
  Pallas kernels  89.7 us (89%)
  other arithmetic  4.98 us (5%)
  matrix products  4.29 us (4%)
    pallas_call x1, Pallas kernels, kernel_shards(): pl.pallas_call(functools.partial(fused, nz, chunk), out_shape=[jax.ShapeD...  89.7 us
    convert_element_type x2, other arithmetic, kernel_shards(): return (image_back[None], text_back[None], hi.astype(f32), ht.astype(f32))  4.98 us
    dot_general x1, matrix products, kernel_shards(): lax.dot_general(pre_i, image_head, NT, preferred_element_type=f32)  2.33 us

profile of v3, /device:TPU:1, one launch (start us, length us, event | category | flops | bytes accessed | tf_op | source)
XLA Modules:
  0.0 100.5 jit_solution(15565023738264480715)
XLA Ops:
  0.6 89.7 %shard_map.93 = (bf16[512,768]{1,0:T(8,128)(2,1)}, bf16[512,768]{1,0:T(8,128)(2,1)}, bf16[1024,768]{1,0:T(8,128)(2,1)}, bf16[768,768]{1,0:T(8,128)(2,1)}) custom-call(bf16[512,1024]{1,0:T(8,128)(2,1)} %bitcast.10, bf16[512,768]{1,0:T(8,128)(2,1)} %bitcast.11, bf16[1024,768]{1,0:T(8,128)(2,1)} %wi_in.1, bf16[768,768]{1,0:T(8,128)(2,1)} %wt_in.1, ...), custom_call_target="tpu_custom_call" | custom-call | tf_op jit(solution)/shard_map/pallas_call | solution.py:378
  90.3 0.0 copy-start.1
  90.3 3.4 %convert_element_type.6 = f32[1024,768]{1,0:T(8,128)} convert(bf16[1024,768]{1,0:T(8,128)(2,1)} %get-tuple-element.10) | non-fusion elementwise | flops 786432 | bytes 4718592 | tf_op jit(solution)/shard_map/convert_element_type | solution.py:407
  93.7 0.0 copy-done.1
  93.7 0.0 copy-start
  93.7 0.0 copy-start.4
  93.7 1.6 %convert_element_type.7 = f32[768,768]{1,0:T(8,128)} convert(bf16[768,768]{1,0:T(8,128)(2,1)S(1)} %copy-done.1) | non-fusion elementwise | flops 589824 | bytes 3538944 | tf_op jit(solution)/shard_map/convert_element_type | solution.py:407
  95.3 0.5 copy-done
  95.9 0.3 copy-done.4
  96.2 0.0 copy-start.2
  96.2 0.0 copy-start.3
  96.2 2.3 %convolution_bitcast_fusion = f32[1,512,1024]{2,1,0:T(8,128)} fusion(bf16[512,768]{1,0:T(8,128)(2,1)S(1)} %copy-done.4, bf16[1024,768]{1,0:T(8,128)(2,1)S(1)} %copy-done), kind=kOutput, calls=%fused_computation | convolution fusion | flops 805306368 | bytes 4456448 | tf_op jit(solution)/shard_map/dot_general | solution.py:405
  98.5 0.0 copy-done.2
  98.5 0.0 copy-done.3
  98.5 2.0 %convolution_bitcast_fusion.1 = f32[1,512,768]{2,1,0:T(8,128)} fusion(bf16[512,768]{1,0:T(8,128)(2,1)S(1)} %copy-done.3, bf16[768,768]{1,0:T(8,128)(2,1)S(1)} %copy-done.2), kind=kOutput, calls=%fused_computation.1 | convolution fusion | flops 603979776 | bytes 3538944 | tf_op jit(solution)/shard_map/dot_general | solution.py:406
Async XLA Ops:
  90.3 3.4 %copy-start.1 = (bf16[768,768]{1,0:T(8,128)(2,1)S(1)}, bf16[768,768]{1,0:T(8,128)(2,1)}, u32[]{:S(2)}) copy-start(bf16[768,768]{1,0:T(8,128)(2,1)} %get-tuple-element.11) | copy-start | bytes 3538948
  93.7 2.1 %copy-start = (bf16[1024,768]{1,0:T(8,128)(2,1)S(1)}, bf16[1024,768]{1,0:T(8,128)(2,1)}, u32[]{:S(2)}) copy-start(bf16[1024,768]{1,0:T(8,128)(2,1)} %wi_in.1) | copy-start | bytes 4718596
  93.7 2.5 %copy-start.4 = (bf16[512,768]{1,0:T(8,128)(2,1)S(1)}, bf16[512,768]{1,0:T(8,128)(2,1)}, u32[]{:S(2)}) copy-start(bf16[512,768]{1,0:T(8,128)(2,1)} %get-tuple-element.8) | copy-start | bytes 2359300
  96.2 2.3 %copy-start.2 = (bf16[768,768]{1,0:T(8,128)(2,1)S(1)}, bf16[768,768]{1,0:T(8,128)(2,1)}, u32[]{:S(2)}) copy-start(bf16[768,768]{1,0:T(8,128)(2,1)} %wt_in.1) | copy-start | bytes 3538948
  96.2 2.3 %copy-start.3 = (bf16[512,768]{1,0:T(8,128)(2,1)S(1)}, bf16[512,768]{1,0:T(8,128)(2,1)}, u32[]{:S(2)}) copy-start(bf16[512,768]{1,0:T(8,128)(2,1)} %get-tuple-element.9) | copy-start | bytes 2359300

commit v4 on v3

--- a/solution.py
+++ b/solution.py
@@ -359,6 +359,13 @@
         copy.wait()
     for copy in started:
         copy.wait_send()
+
+
+def tail(pi, pt, wi, wt, hi, ht, bi, bt, gi, gt):
+    bi[...] = mm(pi[...], wi[...], NT)
+    bt[...] = mm(pt[...], wt[...], NT)
+    gi[...] = hi[...].astype(jnp.float32)
+    gt[...] = ht[...].astype(jnp.float32)
 
 
 def kernel_shards(nz, image_feats, text_feats, image_head, text_head, image_lse, text_lse):
@@ -402,9 +409,28 @@
             collective_id=0, has_side_effects=True, vmem_limit_bytes=60 * 1024 * 1024
         ),
     )(image_feats[0], text_feats[0], image_head, text_head, image_lse, text_lse)
-    image_back = lax.dot_general(pre_i, image_head, NT, preferred_element_type=f32)
-    text_back = lax.dot_general(pre_t, text_head, NT, preferred_element_type=f32)
-    return (image_back[None], text_back[None], hi.astype(f32), ht.astype(f32))
+    steps = 4
+
+    def rows_of(total, width):
+        return pl.BlockSpec((total // steps, width), lambda k: (k, 0))
+
+    def whole(total):
+        return pl.BlockSpec((total, e), lambda k: (0, 0))
+
+    image_back, text_back, image_total, text_total = pl.pallas_call(
+        tail,
+        grid=(steps,),
+        out_shape=[
+            jax.ShapeDtypeStruct((n, di), f32),
+            jax.ShapeDtypeStruct((n, dt), f32),
+            jax.ShapeDtypeStruct((di, e), f32),
+            jax.ShapeDtypeStruct((dt, e), f32),
+        ],
+        in_specs=[rows_of(n, e), rows_of(n, e), whole(di), whole(dt), rows_of(di, e), rows_of(dt, e)],
+        out_specs=[rows_of(n, di), rows_of(n, dt), rows_of(di, e), rows_of(dt, e)],
+        compiler_params=pltpu.CompilerParams(vmem_limit_bytes=60 * 1024 * 1024),
+    )(pre_i, pre_t, image_head, text_head, hi, ht)
+    return (image_back[None], text_back[None], image_total, text_total)
 
 
 def solution(mesh):

time: 101 us -> 99.6 us (0.986)
  Pallas kernels: 89.7 us -> 98.7 us
  other arithmetic: 4.98 us -> 0 us
  matrix products: 4.29 us -> 0 us
    pallas_call x0 -> x1, Pallas kernels: none -> 9.01 us  [kernel_shards(): pl.pallas_call(tail, grid=(steps,), out_shape=[jax.ShapeDtypeStruct((n, d...]
    convert_element_type x2 -> x0, other arithmetic: 4.98 us -> none  [kernel_shards(): return (image_back[None], text_back[None], hi.astype(f32), ht.astype(f32))]
    dot_general x2 -> x0, matrix products: 4.29 us -> none  [the longest x1 2.33 us: kernel_shards(): lax.dot_general(pre_i, image_head, NT, preferred_element_type=f32)]
where the time goes in v4:
time: 99.6 us; the launch traced here: 99.4 us
  Pallas kernels  98.7 us (99%)
    pallas_call x1, Pallas kernels, kernel_shards(): pl.pallas_call(functools.partial(fused, nz, chunk), out_shape=[jax.ShapeD...  89.7 us
    pallas_call x1, Pallas kernels, kernel_shards(): pl.pallas_call(tail, grid=(steps,), out_shape=[jax.ShapeDtypeStruct((n, d...  9.01 us

profile of v4, /device:TPU:1, one launch (start us, length us, event | category | flops | bytes accessed | tf_op | source)
XLA Modules:
  0.0 99.4 jit_solution(11192242996174056343)
XLA Ops:
  0.6 89.7 %shard_map.93 = (bf16[512,768]{1,0:T(8,128)(2,1)}, bf16[512,768]{1,0:T(8,128)(2,1)}, bf16[1024,768]{1,0:T(8,128)(2,1)}, bf16[768,768]{1,0:T(8,128)(2,1)}) custom-call(bf16[512,1024]{1,0:T(8,128)(2,1)} %bitcast.4, bf16[512,768]{1,0:T(8,128)(2,1)} %bitcast.5, bf16[1024,768]{1,0:T(8,128)(2,1)} %wi.1, bf16[768,768]{1,0:T(8,128)(2,1)} %wt.1, f32[1,512]{1,0:T(1,128)} %li.1, ...), custom_call_target="tpu_custom_call" | custom-call | tf_op jit(solution)/shard_map/pallas_call | solution.py:385
  90.3 9.0 %shard_map.94 = (f32[512,1024]{1,0:T(8,128)}, f32[512,768]{1,0:T(8,128)}, f32[1024,768]{1,0:T(8,128)}, f32[768,768]{1,0:T(8,128)}) custom-call(bf16[512,768]{1,0:T(8,128)(2,1)} %get-tuple-element.12.pi, bf16[512,768]{1,0:T(8,128)(2,1)} %get-tuple-element.13.pt, bf16[1024,768]{1,0:T(8,128)(2,1)} %wi.1, bf16[768,768]{1,0:T(8,128)(2,1)} %wt.1, ...), custom_call_target="tpu_custom_call" | custom-call | tf_op jit(solution)/shard_map/pallas_call | solution.py:420
